TPU v7x, 256 devices: a whole 4x4x8 slice. The times are simulated.
256 devices in a mesh: space: 64 (over z, x, core), inst: 4 (over y).
Axes of the slice: x: 4, y: 4, z: 8, core: 2. Of those that a mesh axis runs over, the one named last changes fastest.
Arguments:
- adjoint: float32 [8, 5, 131072], P('inst', None, 'space'), may hold values from -6 to 6
- jac_cell: float32 [8, 5, 5, 131072], P('inst', None, None, 'space'), may hold values from -2.5 to 2.5
- jac_left: float32 [8, 5, 5, 131072], P('inst', None, None, 'space'), may hold values from -2.5 to 2.5
- jac_right: float32 [8, 5, 5, 131072], P('inst', None, None, 'space'), may hold values from -2.5 to 2.5
- volume: float32 [131072], P('space'), may hold values from 0.5 to 2
- normals: float32 [3, 131072], P(None, 'space'), may hold values from -6 to 6
- surface: int32 [131072], P('space'), may hold values 0 or 1
- instance_map: int32 [8], replicated, may hold values from 0 to 7, each once
- mode_shapes: float32 [200, 3, 131072], P(None, None, 'space'), may hold values from -0.01953125 to 0.01953125
- damping: float32 [200], replicated, may hold values from 0.2 to 2
- modal_inverse: float32 [200, 200], replicated, may hold values from -2 to 3
Outputs:
- flow_residual: float32 [8, 5, 131072], P('inst', None, 'space')
- mesh_forcing: float32 [8, 3, 131072], P('inst', None, 'space')
- modal_adjoint: float32 [8, 200], P('inst')
All inputs are finite; a program needn't handle non-finite values. No bound on the sum of `surface` on one device may be relied on, other than what follows from the above.
Results may differ from a plain program's by a relative error of at most 0.000068.
Values sent between devices are 32-bit elements; how exact they have to be, the bound alone decides.
A program may use at most 64 MiB of HBM per device.

v0:
```python
import jax
import jax.numpy as jnp
from jax import lax
from jax.sharding import PartitionSpec as P


def padded_2(shard, sides, width):
    for axis, dim in sides:
        count, length = (lax.axis_size(axis), shard.shape[dim])
        up = [(i, (i + 1) % count) for i in range(count - 1)]
        down = [(j, i) for i, j in up]
        last = lax.slice_in_dim(shard, length - width, length, axis=dim)
        leading = lax.slice_in_dim(shard, 0, width, axis=dim)
        before = lax.ppermute(last, axis, up)
        after = lax.ppermute(leading, axis, down)
        shard = jnp.concatenate([before, shard, after], axis=dim)
    return shard


def coupling_matrix(instance_map):
    count = instance_map.shape[0]
    slots = instance_map.astype(jnp.float32)
    differ = slots[:, None] - slots[None, :]
    angle = jnp.pi * differ / count
    same = differ == 0
    sine = jnp.where(same, 1.0, jnp.sin(angle))
    return jnp.where(same, 0.0, 0.5 * jnp.cos(jnp.pi * differ) * jnp.cos(angle) / sine)


def shards(
    adjoint,
    jac_cell,
    jac_left,
    jac_right,
    volume,
    normals,
    surface,
    instance_map,
    mode_shapes,
    damping,
    modal_inverse,
):
    highest = lax.Precision.HIGHEST
    own_slots = adjoint.shape[0]
    modes = mode_shapes.shape[0]
    first_slot = lax.axis_index("inst") * own_slots
    coupling = coupling_matrix(instance_map)
    own_cols = lax.dynamic_slice_in_dim(coupling, first_slot, own_slots, 1)
    flow = jnp.einsum("sfec,sfc->sec", jac_cell, adjoint, precision=highest)
    from_left = jnp.einsum("sfec,sfc->sec", jac_left, adjoint, precision=highest)
    from_right = jnp.einsum("sfec,sfc->sec", jac_right, adjoint, precision=highest)
    stacked = jnp.stack([from_left, from_right])
    padded = padded_2(stacked, (("space", 3),), 1)
    flow = flow + padded[0, :, :, 2:] + padded[1, :, :, :-2]
    timed = jnp.einsum(
        "ab,aec->bec",
        own_cols,
        lax.all_gather(adjoint, "inst", axis=0, tiled=True),
        precision=highest,
    )
    flow = flow + volume[None, None, :] * timed
    walls = surface.astype(jnp.float32)
    force = (walls[None, :] * flow[:, 4, :])[:, None, :] * normals[None, :, :]
    shapes = mode_shapes.reshape(modes, -1)
    projected = lax.dot_general(
        force.reshape(own_slots, -1),
        shapes,
        (((1,), (1,)), ((), ())),
        precision=highest,
        preferred_element_type=jnp.float32,
    )
    summed = lax.psum(projected, "space")
    gathered = lax.all_gather(summed, "inst", axis=0, tiled=True)
    own_projected = lax.dynamic_slice_in_dim(gathered, first_slot, own_slots, 0)
    modal_rhs = own_projected + damping[None, :] * jnp.dot(own_cols.T, gathered, precision=highest)
    modal_adjoint = jnp.dot(modal_rhs, modal_inverse, precision=highest)
    expanded = jnp.dot(modal_adjoint, shapes, precision=highest).reshape(own_slots, 3, -1)
    mesh_forcing = walls[None, None, :] * expanded
    return (flow, mesh_forcing, modal_adjoint)


def solution(mesh):
    placed = (
        P("inst", None, "space"),
        P("inst", None, None, "space"),
        P("inst", None, None, "space"),
        P("inst", None, None, "space"),
        P("space"),
        P(None, "space"),
        P("space"),
        P(),
        P(None, None, "space"),
        P(),
        P(),
    )
    return jax.shard_map(
        shards,
        mesh=mesh,
        in_specs=placed,
        out_specs=(P("inst", None, "space"), P("inst", None, "space"), P("inst", None)),
        check_vma=False,
    )
```

profile of v0, /device:TPU:8, one launch (start us, length us, event | category | flops | bytes accessed | tf_op | source)
XLA Modules:
  0.0 175.6 jit_solution(5606615448060914393)
XLA Ops:
  0.6 0.0 copy-start
  0.6 0.0 copy-start.3
  0.7 2.1 %multiply_reduce_fusion.2 = (f32[2,2048,5]{1,0,2:T(2,128)S(1)}, f32[2,2048,5]{1,0,2:T(2,128)S(1)}, f32[2,2048,5]{1,0,2:T(2,128)S(1)}) fusion(f32[2,5,5,2048]{3,0,2,1:T(2,128)} %param.12, f32[2,2048,5]{1,0,2:T(2,128)} %bitcast.61, f32[2,5,5,2048]{3,0,2,1:T(2,128)} %param.13, f32[2,5,5,2048]{3,0,2,1:T(2,128)} %param.14), kind=kLoop, calls=%fused_computation.10 | loop fusion | flops 552960 | bytes 1556480 | tf_op jit(solution)/shard_map/sfec,sfc->sec/dot_general | solution.py:49
  2.8 0.1 pad_maximum_fusion.5
  2.9 1.7 collective-permute-start.1
  4.6 1.3 collective-permute-start
  5.9 0.9 copy.16
  6.8 13.6 %all_gather.6 = f32[8,5,2048]{2,1,0:T(8,128)S(1)} all-gather(f32[2,5,2048]{2,1,0:T(8,128)S(1)} %copy.16), channel_id=1, replica_groups=mesh['space'=64,'inst'=4] {'inst'}, dimensions={0}, use_global_device_ids=true | all-gather | bytes 409600 | tf_op jit(solution)/shard_map/all_gather | solution.py:58
  20.5 0.7 convert_element_type.6
  21.1 0.1 fusion.21
  21.3 0.7 convert_element_type.7
  22.0 0.0 collective-permute-done.1
  22.0 0.0 collective-permute-done
  22.0 1.3 fusion.10
  23.3 0.0 copy-start.2
  23.3 5.8 %convolution_bitcast_fusion = f32[2,200]{1,0:T(2,128)S(1)} fusion(f32[200,3,2048]{2,0,1:T(8,128)} %param.19, f32[3,2048]{1,0:T(4,128)} %param.16, f32[2,2048]{1,0:T(2,128)S(1)} %fusion.18), kind=kOutput, calls=%fused_computation.6 | convolution fusion | flops 29503488 | bytes 4957760 | tf_op jit(solution)/shard_map/dot_general | solution.py:65
  29.1 129.9 %psum.7 = f32[2,200]{1,0:T(2,128)S(1)} all-reduce(f32[2,200]{1,0:T(2,128)S(1)} %convolution_bitcast_fusion), channel_id=1, replica_groups=mesh['space'=64,'inst'=4] {'space'}, use_global_device_ids=true, to_apply=%region_0.1 | all-reduce | flops 400 | bytes 3200 | tf_op jit(solution)/shard_map/psum | solution.py:72
  159.1 10.7 %all-gather = f32[4,2,200]{2,1,0:T(2,128)S(1)} all-gather(f32[1,2,200]{2,1,0:T(2,128)S(1)} %bitcast.66), channel_id=1, replica_groups=mesh['space'=64,'inst'=4] {'inst'}, dimensions={0}, use_global_device_ids=true | all-gather | bytes 8000 | tf_op jit(solution)/shard_map/all_gather | solution.py:73
  169.8 0.0 copy-done.3
  169.8 0.1 fusion.6
  169.9 0.0 copy-done
  169.9 0.2 fusion.33
  170.1 0.0 copy-start.1
  170.1 5.5 %fusion.3 = f32[2,3,2048]{2,0,1:T(2,128)} fusion(f32[2048]{0:T(1024)S(1)} %convert_element_type.7, f32[2,200]{1,0:T(2,128)S(1)} %fusion.33, f32[200,3,2048]{2,0,1:T(8,128)} %param.19), kind=kOutput, calls=%fused_computation.4 | convolution fusion | flops 29503488 | bytes 4974144 | tf_op jit(solution)/shard_map/dot_general | solution.py:77
  175.6 0.0 copy-done.2
  175.6 0.0 copy-done.1
  (2 shorter events, 0.0 us)
Async XLA Ops:
  0.6 169.3 %copy-start = (f32[200,200]{1,0:T(8,128)S(1)}, f32[200,200]{1,0:T(8,128)}, u32[]{:S(2)}) copy-start(f32[200,200]{1,0:T(8,128)} %param.21) | copy-start | bytes 480004
  0.6 169.1 %copy-start.3 = (f32[200]{0:T(256)S(1)}, f32[200]{0:T(256)}, u32[]{:S(2)}) copy-start(f32[200]{0:T(256)} %param.20) | copy-start | bytes 2404
  2.9 19.1 %collective-permute-start.1 = (f32[2,2,5,1]{3,1,2,0:T(2,128)S(1)}, f32[2,2,5,1]{3,1,2,0:T(2,128)S(1)}, u32[]{:S(2)}, u32[]{:S(2)}) collective-permute-start(f32[2,2,5,1]{3,1,2,0:T(2,128)S(1)} %get-tuple-element.7), channel_id=1, source_target_pairs={{0,4},{4,8},{8,12},{12,16},{16,20},{20,24},{24,28},{28,32},{32,36}... | collective-permute-start | bytes 248 | tf_op jit(solution)/shard_map/ppermute | solution.py:14
  4.6 17.4 %collective-permute-start = (f32[2,2,5,1]{3,1,2,0:T(2,128)S(1)}, f32[2,2,5,1]{3,1,2,0:T(2,128)S(1)}, u32[]{:S(2)}, u32[]{:S(2)}) collective-permute-start(f32[2,2,5,1]{3,1,2,0:T(2,128)S(1)} %get-tuple-element.6), channel_id=1, source_target_pairs={{4,0},{8,4},{12,8},{16,12},{20,16},{24,20},{28,24},{32,28},{36,32}... | collective-permute-start | bytes 248 | tf_op jit(solution)/shard_map/ppermute | solution.py:15
  23.3 152.3 %copy-start.2 = (f32[2,5,2048]{2,0,1:T(2,128)}, f32[2,5,2048]{2,0,1:T(2,128)S(1)}, u32[]{:S(2)}) copy-start(f32[2,5,2048]{2,0,1:T(2,128)S(1)} %fusion.10) | copy-start | bytes 245764
  170.1 5.5 %copy-start.1 = (f32[2,200]{1,0:T(2,128)}, f32[2,200]{1,0:T(2,128)S(1)}, u32[]{:S(2)}) copy-start(f32[2,200]{1,0:T(2,128)S(1)} %fusion.33) | copy-start | bytes 4804
where the time goes:
time: 176 us
  blocking collectives  154 us (88%)
  matrix products  12.8 us (7%)
  other arithmetic  3.69 us (2%)
  starting transfers between devices  3.02 us (2%)
    psum x1, blocking collectives, shards(): summed = lax.psum(projected, 'space')  130 us
    all_gather x1, blocking collectives, shards(): lax.all_gather(adjoint, 'inst', axis=0, tiled=True)  13.6 us
    all_gather x1, blocking collectives, shards(): gathered = lax.all_gather(summed, 'inst', axis=0, tiled=True)  10.7 us
    dot_general x1, matrix products, shards(): lax.dot_general(force.reshape(own_slots, -1), shapes, (((1,), (1,)), ((),...  5.76 us
    dot_general x1, matrix products, shards(): jnp.dot(modal_adjoint, shapes, precision=highest).reshape(own_slots, 3, -1)  5.45 us
  transfers between devices with their start and end apart: 2, of which 0 were waited for; matrix products, arithmetic and copies ran while one was open for 1% of the time, Pallas kernels for 0%

commit v1 on v0

--- a/solution.py
+++ b/solution.py
@@ -52,12 +52,27 @@
     stacked = jnp.stack([from_left, from_right])
     padded = padded_2(stacked, (("space", 3),), 1)
     flow = flow + padded[0, :, :, 2:] + padded[1, :, :, :-2]
-    timed = jnp.einsum(
+    devices, index = (lax.axis_size("inst"), lax.axis_index("inst"))
+    backward = [(i_2, (i_2 - 1) % devices) for i_2 in range(devices)]
+    width_2 = adjoint.shape[0]
+    held = adjoint
+    total = jnp.einsum(
         "ab,aec->bec",
-        own_cols,
-        lax.all_gather(adjoint, "inst", axis=0, tiled=True),
+        lax.dynamic_slice_in_dim(own_cols, index * width_2, held.shape[0], axis=0),
+        held,
         precision=highest,
     )
+    for step in range(1, devices):
+        held = lax.ppermute(held, "inst", backward)
+        total = total + jnp.einsum(
+            "ab,aec->bec",
+            lax.dynamic_slice_in_dim(
+                own_cols, (index + step) % devices * width_2, held.shape[0], axis=0
+            ),
+            held,
+            precision=highest,
+        )
+    timed = total
     flow = flow + volume[None, None, :] * timed
     walls = surface.astype(jnp.float32)
     force = (walls[None, :] * flow[:, 4, :])[:, None, :] * normals[None, :, :]

time: 176 us -> 176 us (level)
  blocking collectives: 154 us -> 142 us
  waiting for transfers between devices: 0.01 us -> 6.53 us
  starting transfers between devices: 3.02 us -> 7.02 us
  matrix products: 12.8 us -> 15.1 us
    all_gather x1 -> x0, blocking collectives: 13.6 us -> none  [shards(): lax.all_gather(adjoint, 'inst', axis=0, tiled=True)]
    ppermute x0 -> x3, waiting for transfers between devices: none -> 6.52 us  [shards(): held = lax.ppermute(held, 'inst', backward)]
    ppermute x0 -> x3, starting transfers between devices: none -> 4.45 us  [shards(): held = lax.ppermute(held, 'inst', backward)]
    dot_general x1 -> x4, matrix products: 1.31 us -> 3.54 us  [the longest x3 2.18 us: shards(): jnp.einsum('ab,aec->bec', lax.dynamic_slice_in_dim(own_cols, (index + ste...]
    all_gather x1, blocking collectives: 10.7 us -> 12.7 us  [shards(): gathered = lax.all_gather(summed, 'inst', axis=0, tiled=True)]
  transfers between devices with their start and end apart: 2 -> 5, of which waited for: 0 -> 2; matrix products, arithmetic and copies ran while one was open for 1% -> 3% of each run, Pallas kernels for 0% -> 0%
where the time goes in v1:
time: 176 us; the launch traced here: 175 us
  blocking collectives  142 us (81%)
  matrix products  15.1 us (9%)
  starting transfers between devices  7.02 us (4%)
  waiting for transfers between devices  6.53 us (4%)
  other arithmetic  3.69 us (2%)
    psum x1, blocking collectives, shards(): summed = lax.psum(projected, 'space')  130 us
    all_gather x1, blocking collectives, shards(): gathered = lax.all_gather(summed, 'inst', axis=0, tiled=True)  12.7 us
    ppermute x3, waiting for transfers between devices, shards(): held = lax.ppermute(held, 'inst', backward)  6.52 us
    dot_general x1, matrix products, shards(): lax.dot_general(force.reshape(own_slots, -1), shapes, (((1,), (1,)), ((),...  5.76 us
    dot_general x1, matrix products, shards(): jnp.dot(modal_adjoint, shapes, precision=highest).reshape(own_slots, 3, -1)  5.45 us
    ppermute x3, starting transfers between devices, shards(): held = lax.ppermute(held, 'inst', backward)  4.45 us
  transfers between devices with their start and end apart: 5, of which 2 were waited for; matrix products, arithmetic and copies ran while one was open for 3% of the time, Pallas kernels for 0%

profile of v1, /device:TPU:8, one launch (start us, length us, event | category | flops | bytes accessed | tf_op | source)
XLA Modules:
  0.0 175.4 jit_solution(5982157432668248277)
XLA Ops:
  0.6 0.0 copy-start
  0.6 0.0 copy-start.3
  0.7 2.3 %collective-permute-start.2 = (f32[2,5,2048]{2,0,1:T(2,128)}, f32[2,5,2048]{2,0,1:T(2,128)S(1)}, u32[]{:S(2)}, u32[]{:S(2)}) collective-permute-start(f32[2,5,2048]{2,0,1:T(2,128)} %param.11), channel_id=1, source_target_pairs={{0,3},{1,0},{2,1},{3,2},{4,7},{5,4},{6,5},{7,6},{8,11},{9,8},{10,9... | collective-permute-start | bytes 245768 | tf_op jit(solution)/shard_map/ppermute | solution.py:66
  2.9 2.1 %multiply_reduce_fusion.2 = (f32[2,2048,5]{1,0,2:T(2,128)S(1)}, f32[2,2048,5]{1,0,2:T(2,128)S(1)}, f32[2,2048,5]{1,0,2:T(2,128)S(1)}) fusion(f32[2,5,5,2048]{3,0,2,1:T(2,128)} %param.12, f32[2,2048,5]{1,0,2:T(2,128)} %bitcast.74, f32[2,5,5,2048]{3,0,2,1:T(2,128)} %param.13, f32[2,5,5,2048]{3,0,2,1:T(2,128)} %param.14), kind=kLoop, calls=%fused_computation.14 | loop fusion | flops 552960 | bytes 1556480 | tf_op jit(solution)/shard_map/sfec,sfc->sec/dot_general | solution.py:49
  5.0 0.1 pad_maximum_fusion.5
  5.1 1.3 collective-permute-start.1
  6.4 1.3 collective-permute-start
  7.7 0.7 convert_element_type.6
  8.4 0.1 fusion.19
  8.5 1.4 fusion.29
  9.9 0.7 convert_element_type.7
  10.6 0.0 collective-permute-done.2
  10.6 1.4 collective-permute-start.3
  12.1 0.5 convolution_add_fusion.2
  12.6 3.2 %collective-permute-done.3 = f32[2,5,2048]{2,0,1:T(2,128)S(1)} collective-permute-done((f32[2,5,2048]{2,0,1:T(2,128)S(1)}, f32[2,5,2048]{2,0,1:T(2,128)S(1)}, u32[]{:S(2)}, u32[]{:S(2)}) %collective-permute-start.3) | collective-permute-done | bytes 81952 | tf_op jit(solution)/shard_map/ppermute | solution.py:66
  15.8 0.7 collective-permute-start.4
  16.5 0.5 convolution_add_fusion.1
  17.0 0.0 collective-permute-done.1
  17.0 0.0 collective-permute-done
  17.0 3.3 %collective-permute-done.4 = f32[2,5,2048]{2,0,1:T(2,128)S(1)} collective-permute-done((f32[2,5,2048]{2,0,1:T(2,128)S(1)}, f32[2,5,2048]{2,0,1:T(2,128)S(1)}, u32[]{:S(2)}, u32[]{:S(2)}) %collective-permute-start.4) | collective-permute-done | bytes 81952 | tf_op jit(solution)/shard_map/ppermute | solution.py:66
  20.3 1.2 fusion.4
  21.6 0.0 copy-start.2
  21.6 5.8 %convolution_bitcast_fusion = f32[2,200]{1,0:T(2,128)S(1)} fusion(f32[200,3,2048]{2,0,1:T(8,128)} %param.19, f32[3,2048]{1,0:T(4,128)} %param.16, f32[2,2048]{1,0:T(2,128)S(1)} %fusion.16), kind=kOutput, calls=%fused_computation.10 | convolution fusion | flops 29503488 | bytes 4957760 | tf_op jit(solution)/shard_map/dot_general | solution.py:80
  27.4 129.5 %psum.7 = f32[2,200]{1,0:T(2,128)S(1)} all-reduce(f32[2,200]{1,0:T(2,128)S(1)} %convolution_bitcast_fusion), channel_id=1, replica_groups=mesh['space'=64,'inst'=4] {'space'}, use_global_device_ids=true, to_apply=%region_0.1 | all-reduce | flops 400 | bytes 3200 | tf_op jit(solution)/shard_map/psum | solution.py:87
  156.9 12.7 %all-gather = f32[4,2,200]{2,1,0:T(2,128)S(1)} all-gather(f32[1,2,200]{2,1,0:T(2,128)S(1)} %bitcast.79), channel_id=1, replica_groups=mesh['space'=64,'inst'=4] {'inst'}, dimensions={0}, use_global_device_ids=true | all-gather | bytes 8000 | tf_op jit(solution)/shard_map/all_gather | solution.py:88
  169.6 0.0 copy-done.3
  169.6 0.1 fusion.8
  169.8 0.0 copy-done
  169.8 0.2 fusion.37
  170.0 0.0 copy-start.1
  170.0 5.5 %fusion.5 = f32[2,3,2048]{2,0,1:T(2,128)} fusion(f32[2048]{0:T(1024)S(1)} %convert_element_type.7, f32[2,200]{1,0:T(2,128)S(1)} %fusion.37, f32[200,3,2048]{2,0,1:T(8,128)} %param.19), kind=kOutput, calls=%fused_computation.8 | convolution fusion | flops 29503488 | bytes 4974144 | tf_op jit(solution)/shard_map/dot_general | solution.py:92
  175.4 0.0 copy-done.2
  175.4 0.0 copy-done.1
  (2 shorter events, 0.0 us)
Async XLA Ops:
  0.6 169.1 %copy-start = (f32[200,200]{1,0:T(8,128)S(1)}, f32[200,200]{1,0:T(8,128)}, u32[]{:S(2)}) copy-start(f32[200,200]{1,0:T(8,128)} %param.21) | copy-start | bytes 480004
  0.6 169.0 %copy-start.3 = (f32[200]{0:T(256)S(1)}, f32[200]{0:T(256)}, u32[]{:S(2)}) copy-start(f32[200]{0:T(256)} %param.20) | copy-start | bytes 2404
  0.7 10.0 %collective-permute-start.2 = (f32[2,5,2048]{2,0,1:T(2,128)}, f32[2,5,2048]{2,0,1:T(2,128)S(1)}, u32[]{:S(2)}, u32[]{:S(2)}) collective-permute-start(f32[2,5,2048]{2,0,1:T(2,128)} %param.11), channel_id=1, source_target_pairs={{0,3},{1,0},{2,1},{3,2},{4,7},{5,4},{6,5},{7,6},{8,11},{9,8},{10,9... | collective-permute-start | bytes 245768 | tf_op jit(solution)/shard_map/ppermute | solution.py:66
  5.1 11.9 %collective-permute-start.1 = (f32[2,2,5,1]{3,1,2,0:T(2,128)S(1)}, f32[2,2,5,1]{3,1,2,0:T(2,128)S(1)}, u32[]{:S(2)}, u32[]{:S(2)}) collective-permute-start(f32[2,2,5,1]{3,1,2,0:T(2,128)S(1)} %get-tuple-element.7), channel_id=1, source_target_pairs={{0,4},{4,8},{8,12},{12,16},{16,20},{20,24},{24,28},{28,32},{32,36}... | collective-permute-start | bytes 248 | tf_op jit(solution)/shard_map/ppermute | solution.py:14
  6.4 10.6 %collective-permute-start = (f32[2,2,5,1]{3,1,2,0:T(2,128)S(1)}, f32[2,2,5,1]{3,1,2,0:T(2,128)S(1)}, u32[]{:S(2)}, u32[]{:S(2)}) collective-permute-start(f32[2,2,5,1]{3,1,2,0:T(2,128)S(1)} %get-tuple-element.6), channel_id=1, source_target_pairs={{4,0},{8,4},{12,8},{16,12},{20,16},{24,20},{28,24},{32,28},{36,32}... | collective-permute-start | bytes 248 | tf_op jit(solution)/shard_map/ppermute | solution.py:15
  10.6 5.2 %collective-permute-start.3 = (f32[2,5,2048]{2,0,1:T(2,128)S(1)}, f32[2,5,2048]{2,0,1:T(2,128)S(1)}, u32[]{:S(2)}, u32[]{:S(2)}) collective-permute-start(f32[2,5,2048]{2,0,1:T(2,128)S(1)} %collective-permute-done.2), channel_id=1, source_target_pairs={{0,3},{1,0},{2,1},{3,2},{4,7},{5,4},{6,5},{7,6},{8,11},{9,8},{10,9... | collective-permute-start | bytes 245768 | tf_op jit(solution)/shard_map/ppermute | solution.py:66
  15.8 4.5 %collective-permute-start.4 = (f32[2,5,2048]{2,0,1:T(2,128)S(1)}, f32[2,5,2048]{2,0,1:T(2,128)S(1)}, u32[]{:S(2)}, u32[]{:S(2)}) collective-permute-start(f32[2,5,2048]{2,0,1:T(2,128)S(1)} %collective-permute-done.3), channel_id=1, source_target_pairs={{0,3},{1,0},{2,1},{3,2},{4,7},{5,4},{6,5},{7,6},{8,11},{9,8},{10,9... | collective-permute-start | bytes 245768 | tf_op jit(solution)/shard_map/ppermute | solution.py:66
  21.6 153.9 %copy-start.2 = (f32[2,5,2048]{2,0,1:T(2,128)}, f32[2,5,2048]{2,0,1:T(2,128)S(1)}, u32[]{:S(2)}) copy-start(f32[2,5,2048]{2,0,1:T(2,128)S(1)} %fusion.4) | copy-start | bytes 245764
  170.0 5.5 %copy-start.1 = (f32[2,200]{1,0:T(2,128)}, f32[2,200]{1,0:T(2,128)S(1)}, u32[]{:S(2)}) copy-start(f32[2,200]{1,0:T(2,128)S(1)} %fusion.37) | copy-start | bytes 4804
